TPU v7x, 256 devices: a whole 4x4x8 slice. The times are simulated.
256 devices in a mesh: prow: 32 (over z, y), pcol: 8 (over x, core).
Axes of the slice: x: 4, y: 4, z: 8, core: 2. Of those that a mesh axis runs over, the one named last changes fastest.
Arguments:
- right_side: bfloat16 [3, 32, 256, 128], P(None, 'prow'), may hold values from -6 to 6
- lower_blocks: bfloat16 [3, 32, 256, 8192], P(None, 'prow', None, 'pcol'), may hold values from -0.0625 to 0.0625
- upper_blocks: bfloat16 [3, 32, 256, 8192], P(None, 'prow', None, 'pcol'), may hold values from -0.0625 to 0.0625
- lower_inverse: bfloat16 [3, 32, 256, 256], P(None, 'prow'), as said below
- upper_inverse: bfloat16 [3, 32, 256, 256], P(None, 'prow'), as said below
- pattern: int32 [3, 32, 32], replicated, may hold values 0 or 1
Outputs:
- solution: bfloat16 [3, 32, 256, 128], P(None, 'prow')
Inputs may be any that keep to these rules, and one draw needn't show every extreme that they name: `lower_inverse`: each block is lower triangular with its diagonal between 0.6 and 1.4. `upper_inverse`: each block is upper triangular with its diagonal between 0.6 and 1.4.
All inputs are finite; a program needn't handle non-finite values.
Results may differ from a plain program's by a relative error of at most 0.007.
Values may be sent and summed in bfloat16 or wider, within the bound.
A program may use at most 64 MiB of HBM per device.

v0:
```python
import jax
import jax.numpy as jnp
from jax import lax
from jax.sharding import PartitionSpec as P


def pair_index(later, earlier):
    return later * (later - 1) // 2 + earlier


def settle(partial_value, base_rhs, inverse):
    matrix = inverse.astype(jnp.float32)
    if partial_value is None:
        return jnp.dot(matrix, base_rhs, precision=lax.Precision.HIGHEST).astype(jnp.bfloat16)
    summed = lax.psum(partial_value, "pcol")
    return jnp.dot(matrix, base_rhs - summed, precision=lax.Precision.HIGHEST).astype(jnp.bfloat16)


def collect(values, first_col, group_size):
    gathered = lax.all_gather(values[None], "prow", axis=0, tiled=True)
    return lax.dynamic_slice_in_dim(gathered, first_col, group_size, 0)


def body(right_side, lower_blocks, upper_blocks, lower_inverse, upper_inverse, pattern):
    levels = right_side.shape[0]
    block_size = right_side.shape[2]
    width_cols = right_side.shape[3]
    group_size = lower_blocks.shape[3] // block_size
    row_index = lax.axis_index("prow")
    col_index = lax.axis_index("pcol")
    first_col = col_index * group_size
    solved = [None] * levels
    fetched = [None] * levels
    for level_now in range(levels):
        partial_value = None
        for earlier in range(level_now):
            pair_now = pair_index(level_now, earlier)
            keep_mask = lax.dynamic_slice(
                pattern[pair_now], (row_index, first_col), (1, group_size)
            )[0]
            masked = fetched[earlier] * keep_mask.astype(jnp.bfloat16)[:, None, None]
            product = jnp.dot(
                lower_blocks[pair_now, 0],
                masked.reshape(group_size * block_size, width_cols),
                preferred_element_type=jnp.float32,
            )
            partial_value = product if partial_value is None else partial_value + product
        solved[level_now] = settle(
            partial_value, right_side[level_now, 0].astype(jnp.float32), lower_inverse[level_now, 0]
        )
        if level_now + 1 < levels:
            fetched[level_now] = collect(solved[level_now], first_col, group_size)
    results = [None] * levels
    fetched = [None] * levels
    for level_now in reversed(range(levels)):
        partial_value = None
        for later in range(level_now + 1, levels):
            pair_now = pair_index(later, level_now)
            keep_mask = lax.dynamic_slice(
                pattern[pair_now], (first_col, row_index), (group_size, 1)
            )[:, 0]
            masked = fetched[later] * keep_mask.astype(jnp.bfloat16)[:, None, None]
            product = jnp.dot(
                upper_blocks[pair_now, 0],
                masked.reshape(group_size * block_size, width_cols),
                preferred_element_type=jnp.float32,
            )
            partial_value = product if partial_value is None else partial_value + product
        results[level_now] = settle(
            partial_value, solved[level_now].astype(jnp.float32), upper_inverse[level_now, 0]
        )
        if level_now > 0:
            fetched[level_now] = collect(results[level_now], first_col, group_size)
    return jnp.stack(results)[:, None]


def solution(mesh):
    placed = (
        P(None, "prow", None, None),
        P(None, "prow", None, "pcol"),
        P(None, "prow", None, "pcol"),
        P(None, "prow", None, None),
        P(None, "prow", None, None),
        P(),
    )
    return jax.shard_map(
        body, mesh=mesh, in_specs=placed, out_specs=P(None, "prow", None, None), check_vma=False
    )
```

profile of v0, /device:TPU:8, one launch (start us, length us, event | category | flops | bytes accessed | tf_op | source)
XLA Modules:
  0.0 597.5 jit_solution(6616621899532533295)
XLA Ops:
  6.5 1.8 convolution_convert_fusion.5
  8.3 0.0 all-gather.9.cloned.1.call-update
  8.3 0.0 all-reduce.5.cloned.1.call-start
  8.4 0.8 fusion.52
  9.2 0.1 fusion.47
  9.2 80.3 %all-gather.9.cloned.1.call-done = bf16[8192,128]{1,0:T(8,128)(2,1)} async-done(((bf16[256,128]{1,0:T(8,128)(2,1)}), bf16[8192,128]{1,0:T(8,128)(2,1)}) %all-gather.9.cloned.1.call-update) | async-done | bytes 2097168 | tf_op jit(solution)/shard_map/all_gather | solution.py:20
  89.5 1.1 dynamic-slice_multiply_fusion.2
  90.6 2.0 convolution_bitcast_fusion
  92.6 0.0 all-reduce.5.cloned.1.call-update
  92.6 0.0 all-gather.11.cloned.1.call-start
  92.7 63.6 %all-reduce.5.cloned.1.call-done = f32[256,128]{1,0:T(8,128)} async-done(((f32[256,128]{1,0:T(8,128)}), f32[256,128]{1,0:T(8,128)}) %all-reduce.5.cloned.1.call-update) | async-done | bytes 131088 | tf_op jit(solution)/shard_map/psum | solution.py:15
  156.2 1.8 fusion.2
  158.1 0.0 all-gather.11.cloned.1.call-update
  158.1 0.0 all-reduce.7.cloned.1.call-start
  158.2 0.1 fusion.51
  158.2 74.0 %all-gather.11.cloned.1.call-done = bf16[8192,128]{0,1:T(8,128)(2,1)} async-done(((bf16[256,128]{0,1:T(8,128)(2,1)}), bf16[8192,128]{0,1:T(8,128)(2,1)}) %all-gather.11.cloned.1.call-update) | async-done | bytes 2097168 | tf_op jit(solution)/shard_map/all_gather | solution.py:20
  232.2 2.3 copy.8
  234.5 0.2 dynamic-slice_multiply_fusion.1
  234.8 0.3 fusion.8
  235.1 0.9 fusion
  236.0 0.0 all-reduce.7.cloned.1.call-update
  236.1 0.0 all-gather.13.cloned.1.call-start
  236.1 64.4 %all-reduce.7.cloned.1.call-done = f32[256,128]{1,0:T(8,128)} async-done(((f32[256,128]{1,0:T(8,128)}), f32[256,128]{1,0:T(8,128)}) %all-reduce.7.cloned.1.call-update) | async-done | bytes 131088 | tf_op jit(solution)/shard_map/psum | solution.py:15
  300.5 1.2 convolution_convert_fusion.3
  301.7 0.8 convolution_convert_fusion.2
  302.5 0.0 all-gather.13.cloned.1.call-update
  302.5 0.0 all-reduce.9.cloned.1.call-start
  302.6 0.2 fusion.45
  302.8 0.2 fusion.43
  303.0 73.3 %all-gather.13.cloned.1.call-done = bf16[8192,128]{0,1:T(8,128)(2,1)} async-done(((bf16[256,128]{0,1:T(8,128)(2,1)}), bf16[8192,128]{0,1:T(8,128)(2,1)}) %all-gather.13.cloned.1.call-update) | async-done | bytes 2097168 | tf_op jit(solution)/shard_map/all_gather | solution.py:20
  376.3 2.3 copy.10
  378.6 0.3 dynamic-slice_multiply_fusion.4
  378.9 1.0 convolution_bitcast_fusion.1
  379.9 0.0 all-reduce.9.cloned.1.call-update
  379.9 0.0 all-gather.15.cloned.1.call-start
  380.0 64.4 %all-reduce.9.cloned.1.call-done = f32[256,128]{0,1:T(8,128)} async-done(((f32[256,128]{0,1:T(8,128)}), f32[256,128]{0,1:T(8,128)}) %all-reduce.9.cloned.1.call-update) | async-done | bytes 131088 | tf_op jit(solution)/shard_map/psum | solution.py:15
  444.3 1.8 convolution_convert_fusion.1
  446.2 0.0 all-gather.15.cloned.1.call-update
  446.2 0.0 all-reduce.11.cloned.1.call-start
  446.3 74.0 %all-gather.15.cloned.1.call-done = bf16[8192,128]{0,1:T(8,128)(2,1)} async-done(((bf16[256,128]{0,1:T(8,128)(2,1)}), bf16[8192,128]{0,1:T(8,128)(2,1)}) %all-gather.15.cloned.1.call-update) | async-done | bytes 2097168 | tf_op jit(solution)/shard_map/all_gather | solution.py:20
  520.3 2.2 copy.12
  522.5 0.2 dynamic-slice_multiply_fusion
  522.8 0.3 fusion.5
  523.1 1.0 fusion.1
  524.0 0.0 all-reduce.11.cloned.1.call-update
  524.0 64.5 %all-reduce.11.cloned.1.call-done = f32[256,128]{1,0:T(8,128)} async-done(((f32[256,128]{1,0:T(8,128)}), f32[256,128]{1,0:T(8,128)}) %all-reduce.11.cloned.1.call-update) | async-done | bytes 131088 | tf_op jit(solution)/shard_map/psum | solution.py:15
  588.6 1.2 fusion.3
  589.8 0.8 copy.7
  (24 shorter events, 0.2 us)
Async XLA Ops:
  6.5 149.7 %copy-start.7 = (bf16[3,1,256,256]{3,2,1,0:T(8,128)(2,1)S(1)}, bf16[3,1,256,256]{3,2,1,0:T(8,128)(2,1)}, u32[]{:S(2)}) copy-start(bf16[3,1,256,256]{3,2,1,0:T(8,128)(2,1)} %param.9) | copy-start | bytes 1179652
  6.5 149.7 %copy-start.8 = (bf16[3,1,256,128]{3,2,1,0:T(8,128)(2,1)S(1)}, bf16[3,1,256,128]{3,2,1,0:T(8,128)(2,1)}, u32[]{:S(2)}) copy-start(bf16[3,1,256,128]{3,2,1,0:T(8,128)(2,1)} %param.6) | copy-start | bytes 589828
  6.5 83.0 %all-gather.9.cloned.1.call-start = ((), (), s32[]{:S(2)}) async-start(), calls=%async_computation.4 | async-start | bytes 2162688 | tf_op jit(solution)/shard_map/all_gather | solution.py:20
  8.3 147.9 %all-reduce.5.cloned.1.call-start = ((), (), s32[]{:S(2)}) async-start(), calls=%async_computation | async-start | bytes 262144 | tf_op jit(solution)/shard_map/psum | solution.py:15
  92.6 139.6 %all-gather.11.cloned.1.call-start = ((), (), s32[]{:S(2)}) async-start(), calls=%async_computation.5 | async-start | bytes 2162688 | tf_op jit(solution)/shard_map/all_gather | solution.py:20
  158.1 142.4 %all-reduce.7.cloned.1.call-start = ((), (), s32[]{:S(2)}) async-start(), calls=%async_computation.1 | async-start | bytes 262144 | tf_op jit(solution)/shard_map/psum | solution.py:15
  232.2 2.6 copy-start.1
  234.7 67.0 %copy-start.5 = (bf16[3,1,256,256]{3,2,1,0:T(8,128)(2,1)S(1)}, bf16[3,1,256,256]{3,2,1,0:T(8,128)(2,1)}, u32[]{:S(2)}) copy-start(bf16[3,1,256,256]{3,2,1,0:T(8,128)(2,1)} %param.10) | copy-start | bytes 1179652
  236.1 140.2 %all-gather.13.cloned.1.call-start = ((), (), s32[]{:S(2)}) async-start(), calls=%async_computation.6 | async-start | bytes 2162688 | tf_op jit(solution)/shard_map/all_gather | solution.py:20
  302.5 141.8 %all-reduce.9.cloned.1.call-start = ((), (), s32[]{:S(2)}) async-start(), calls=%async_computation.2 | async-start | bytes 262144 | tf_op jit(solution)/shard_map/psum | solution.py:15
  376.3 2.6 copy-start
  378.6 65.8 %copy-start.3 = (bf16[256,128]{0,1:T(8,128)(2,1)S(1)}, bf16[256,128]{0,1:T(8,128)(2,1)}, u32[]{:S(2)}) copy-start(bf16[256,128]{0,1:T(8,128)(2,1)} %fusion.2) | copy-start | bytes 196612
  379.9 140.4 %all-gather.15.cloned.1.call-start = ((), (), s32[]{:S(2)}) async-start(), calls=%async_computation.7 | async-start | bytes 2162688 | tf_op jit(solution)/shard_map/all_gather | solution.py:20
  446.2 142.4 %all-reduce.11.cloned.1.call-start = ((), (), s32[]{:S(2)}) async-start(), calls=%async_computation.3 | async-start | bytes 262144 | tf_op jit(solution)/shard_map/psum | solution.py:15
  522.5 66.1 %copy-start.6 = (bf16[256,128]{1,0:T(8,128)(2,1)S(1)}, bf16[256,128]{1,0:T(8,128)(2,1)}, u32[]{:S(2)}) copy-start(bf16[256,128]{1,0:T(8,128)(2,1)} %convolution_convert_fusion.5) | copy-start | bytes 196612
  522.7 67.1 %copy-start.2 = (bf16[128,256]{1,0:T(8,128)(2,1)S(1)}, bf16[128,256]{1,0:T(8,128)(2,1)}, u32[]{:S(2)}) copy-start(bf16[128,256]{1,0:T(8,128)(2,1)} %convolution_convert_fusion.2) | copy-start | bytes 196612
  522.7 67.1 %copy-start.4 = (bf16[128,256]{1,0:T(8,128)(2,1)S(1)}, bf16[128,256]{1,0:T(8,128)(2,1)}, u32[]{:S(2)}) copy-start(bf16[128,256]{1,0:T(8,128)(2,1)} %convolution_convert_fusion.1) | copy-start | bytes 196612
Sparse Core Ops, SparseCore 0:
  9.9 79.5 all-gather.8
  92.7 63.4 all-reduce.4
  158.7 73.4 all-gather.10
  236.2 64.2 all-reduce.6
  302.8 73.4 all-gather.12
  380.0 64.2 all-reduce.8
  446.8 73.4 all-gather.14
  524.2 64.3 all-reduce.10
where the time goes:
time: 598 us; the launch traced here: 597 us
  waiting for transfers between devices  558 us (93%)
  matrix products  14.1 us (2%)
  between operations  13.7 us (2%)
  local copies, waits for them, and re-layouts  8.51 us (1%)
    all_gather x4, waiting for transfers between devices, collect(): gathered = lax.all_gather(values[None], 'prow', axis=0, tiled=True)  302 us
    psum x4, waiting for transfers between devices, settle(): summed = lax.psum(partial_value, 'pcol')  257 us
  transfers between devices with their start and end apart: 8, of which 8 were waited for; matrix products, arithmetic and copies ran while one was open for 0% of the time, Pallas kernels for 0%

commit v1 on v0

--- a/solution.py
+++ b/solution.py
@@ -17,7 +17,8 @@
 
 
 def collect(values, first_col, group_size):
-    gathered = lax.all_gather(values[None], "prow", axis=0, tiled=True)
+    copies = jnp.concatenate([values[None]] * lax.axis_size("prow"), axis=0)
+    gathered = lax.all_to_all(copies, "prow", 0, 0, tiled=True)
     return lax.dynamic_slice_in_dim(gathered, first_col, group_size, 0)
 
 

time: 598 us -> 525 us (0.88)
  waiting for transfers between devices: 558 us -> 442 us
  starting transfers between devices: 0.3 us -> 42.5 us
    all_gather x4 -> x0, waiting for transfers between devices: 302 us -> none  [collect(): gathered = lax.all_gather(values[None], 'prow', axis=0, tiled=True)]
    all_to_all x0 -> x4, waiting for transfers between devices: none -> 190 us  [collect(): gathered = lax.all_to_all(copies, 'prow', 0, 0, tiled=True)]
    all_to_all x0 -> x4, starting transfers between devices: none -> 42.3 us  [collect(): gathered = lax.all_to_all(copies, 'prow', 0, 0, tiled=True)]
    concatenate x0 -> x4, local copies, waits for them, and re-layouts: none -> 7.31 us  [collect(): copies = jnp.concatenate([values[None]] * lax.axis_size('prow'), axis=0)]
    unnamed x25 -> x6, local copies, waits for them, and re-layouts: 6.93 us -> 0.02 us
where the time goes in v1:
time: 525 us; the launch traced here: 524 us
  waiting for transfers between devices  442 us (84%)
  starting transfers between devices  42.5 us (8%)
  matrix products  16.7 us (3%)
  between operations  13.3 us (3%)
  local copies, waits for them, and re-layouts  8.48 us (2%)
    psum x4, waiting for transfers between devices, settle(): summed = lax.psum(partial_value, 'pcol')  252 us
    all_to_all x4, waiting for transfers between devices, collect(): gathered = lax.all_to_all(copies, 'prow', 0, 0, tiled=True)  190 us
    all_to_all x4, starting transfers between devices, collect(): gathered = lax.all_to_all(copies, 'prow', 0, 0, tiled=True)  42.3 us
  transfers between devices with their start and end apart: 8, of which 8 were waited for; matrix products, arithmetic and copies ran while one was open for 0% of the time, Pallas kernels for 0%

profile of v1, /device:TPU:8, one launch (start us, length us, event | category | flops | bytes accessed | tf_op | source)
XLA Modules:
  0.0 524.2 jit_solution(3702854145263709305)
XLA Ops:
  6.5 1.1 convolution_convert_fusion.5
  7.6 1.8 concatenate.12
  9.4 11.8 %all-to-all-start = ((bf16[32,256,128]{2,1,0:T(8,128)(2,1)}), bf16[32,256,128]{2,1,0:T(8,128)(2,1)S(1)}, u32[]{:S(2)}, u32[]{:S(2)}) async-start(bf16[32,256,128]{2,1,0:T(8,128)(2,1)} %concatenate.12), calls=%async_computation | async-start | bytes 4194304 | tf_op jit(solution)/shard_map/all_to_all | solution.py:21
  21.3 0.0 all-reduce.5.cloned.1.call-start
  21.4 0.1 fusion.47
  21.5 49.1 %all-to-all-done = bf16[32,256,128]{2,1,0:T(8,128)(2,1)S(1)} async-done(((bf16[32,256,128]{2,1,0:T(8,128)(2,1)}), bf16[32,256,128]{2,1,0:T(8,128)(2,1)S(1)}, u32[]{:S(2)}, u32[]{:S(2)}) %all-to-all-start) | async-done | bytes 2097184 | tf_op jit(solution)/shard_map/all_to_all | solution.py:21
  70.5 0.1 dynamic-slice_multiply_fusion.5
  70.6 2.0 convolution_bitcast_fusion
  72.6 0.0 all-reduce.5.cloned.1.call-update
  72.6 63.1 %all-reduce.5.cloned.1.call-done = f32[256,128]{1,0:T(8,128)} async-done(((f32[256,128]{1,0:T(8,128)}), f32[256,128]{1,0:T(8,128)}) %all-reduce.5.cloned.1.call-update) | async-done | bytes 131088 | tf_op jit(solution)/shard_map/psum | solution.py:15
  135.8 1.2 fusion.2
  137.0 0.1 copy.7
  137.1 1.8 concatenate.13
  138.9 10.2 %all-to-all-start.1 = ((bf16[32,256,128]{2,1,0:T(8,128)(2,1)}), bf16[32,256,128]{2,1,0:T(8,128)(2,1)S(1)}, u32[]{:S(2)}, u32[]{:S(2)}) async-start(bf16[32,256,128]{2,1,0:T(8,128)(2,1)} %concatenate.13), calls=%async_computation.1 | async-start | bytes 4194304 | tf_op jit(solution)/shard_map/all_to_all | solution.py:21
  149.1 0.0 all-reduce.7.cloned.1.call-start
  149.1 0.1 fusion.51
  149.2 1.3 fusion.9
  150.5 46.2 %all-to-all-done.1 = bf16[32,256,128]{2,1,0:T(8,128)(2,1)S(1)} async-done(((bf16[32,256,128]{2,1,0:T(8,128)(2,1)}), bf16[32,256,128]{2,1,0:T(8,128)(2,1)S(1)}, u32[]{:S(2)}, u32[]{:S(2)}) %all-to-all-start.1) | async-done | bytes 2097184 | tf_op jit(solution)/shard_map/all_to_all | solution.py:21
  196.7 0.1 dynamic-slice_multiply_fusion.1
  196.8 2.0 fusion.1
  198.8 0.0 all-reduce.7.cloned.1.call-update
  198.8 63.0 %all-reduce.7.cloned.1.call-done = f32[256,128]{1,0:T(8,128)} async-done(((f32[256,128]{1,0:T(8,128)}), f32[256,128]{1,0:T(8,128)}) %all-reduce.7.cloned.1.call-update) | async-done | bytes 131088 | tf_op jit(solution)/shard_map/psum | solution.py:15
  261.8 1.2 convolution_convert_fusion.3
  263.1 0.2 convolution_convert_fusion.2
  263.3 0.1 copy.8
  263.4 1.8 concatenate.14
  265.2 10.2 %all-to-all-start.2 = ((bf16[32,256,128]{2,1,0:T(8,128)(2,1)}), bf16[32,256,128]{2,1,0:T(8,128)(2,1)S(1)}, u32[]{:S(2)}, u32[]{:S(2)}) async-start(bf16[32,256,128]{2,1,0:T(8,128)(2,1)} %concatenate.14), calls=%async_computation.2 | async-start | bytes 4194304 | tf_op jit(solution)/shard_map/all_to_all | solution.py:21
  275.4 0.0 all-reduce.9.cloned.1.call-start
  275.4 0.2 fusion.43
  275.7 47.4 %all-to-all-done.2 = bf16[32,256,128]{2,1,0:T(8,128)(2,1)S(1)} async-done(((bf16[32,256,128]{2,1,0:T(8,128)(2,1)}), bf16[32,256,128]{2,1,0:T(8,128)(2,1)S(1)}, u32[]{:S(2)}, u32[]{:S(2)}) %all-to-all-start.2) | async-done | bytes 2097184 | tf_op jit(solution)/shard_map/all_to_all | solution.py:21
  323.0 0.1 dynamic-slice_multiply_fusion.2
  323.1 2.0 convolution_bitcast_fusion.1
  325.1 0.0 all-reduce.9.cloned.1.call-update
  325.2 63.0 %all-reduce.9.cloned.1.call-done = f32[256,128]{0,1:T(8,128)} async-done(((f32[256,128]{0,1:T(8,128)}), f32[256,128]{0,1:T(8,128)}) %all-reduce.9.cloned.1.call-update) | async-done | bytes 131088 | tf_op jit(solution)/shard_map/psum | solution.py:15
  388.2 1.2 convolution_convert_fusion.1
  389.4 0.1 copy.9
  389.5 1.8 concatenate.15
  391.3 10.2 %all-to-all-start.3 = ((bf16[32,256,128]{2,1,0:T(8,128)(2,1)}), bf16[32,256,128]{2,1,0:T(8,128)(2,1)S(1)}, u32[]{:S(2)}, u32[]{:S(2)}) async-start(bf16[32,256,128]{2,1,0:T(8,128)(2,1)} %concatenate.15), calls=%async_computation.3 | async-start | bytes 4194304 | tf_op jit(solution)/shard_map/all_to_all | solution.py:21
  401.5 0.0 all-reduce.11.cloned.1.call-start
  401.5 0.2 fusion.44
  401.7 47.4 %all-to-all-done.3 = bf16[32,256,128]{2,1,0:T(8,128)(2,1)S(1)} async-done(((bf16[32,256,128]{2,1,0:T(8,128)(2,1)}), bf16[32,256,128]{2,1,0:T(8,128)(2,1)S(1)}, u32[]{:S(2)}, u32[]{:S(2)}) %all-to-all-start.3) | async-done | bytes 2097184 | tf_op jit(solution)/shard_map/all_to_all | solution.py:21
  449.1 0.1 dynamic-slice_multiply_fusion
  449.2 1.3 fusion.5
  450.5 2.0 fusion
  452.5 0.0 all-reduce.11.cloned.1.call-update
  452.5 63.0 %all-reduce.11.cloned.1.call-done = f32[256,128]{1,0:T(8,128)} async-done(((f32[256,128]{1,0:T(8,128)}), f32[256,128]{1,0:T(8,128)}) %all-reduce.11.cloned.1.call-update) | async-done | bytes 131088 | tf_op jit(solution)/shard_map/psum | solution.py:15
  515.6 1.2 fusion.3
  516.8 0.8 copy.10
  (8 shorter events, 0.0 us)
Async XLA Ops:
  9.4 11.9 %copy-start.2 = (s32[3,32,32]{2,1,0:T(8,128)S(1)}, s32[3,32,32]{2,1,0:T(8,128)}, u32[]{:S(2)}) copy-start(s32[3,32,32]{2,1,0:T(8,128)} %param.11) | copy-start | bytes 36868
  9.4 61.1 %all-to-all-start = ((bf16[32,256,128]{2,1,0:T(8,128)(2,1)}), bf16[32,256,128]{2,1,0:T(8,128)(2,1)S(1)}, u32[]{:S(2)}, u32[]{:S(2)}) async-start(bf16[32,256,128]{2,1,0:T(8,128)(2,1)} %concatenate.12), calls=%async_computation | async-start | bytes 4194304 | tf_op jit(solution)/shard_map/all_to_all | solution.py:21
  21.3 114.5 %copy-start.1 = (bf16[3,1,256,256]{3,2,1,0:T(8,128)(2,1)S(1)}, bf16[3,1,256,256]{3,2,1,0:T(8,128)(2,1)}, u32[]{:S(2)}) copy-start(bf16[3,1,256,256]{3,2,1,0:T(8,128)(2,1)} %param.9) | copy-start | bytes 1179652
  21.3 114.5 %all-reduce.5.cloned.1.call-start = ((), (), s32[]{:S(2)}) async-start(), calls=%async_computation.4 | async-start | bytes 262144 | tf_op jit(solution)/shard_map/psum | solution.py:15
  138.9 57.8 %all-to-all-start.1 = ((bf16[32,256,128]{2,1,0:T(8,128)(2,1)}), bf16[32,256,128]{2,1,0:T(8,128)(2,1)S(1)}, u32[]{:S(2)}, u32[]{:S(2)}) async-start(bf16[32,256,128]{2,1,0:T(8,128)(2,1)} %concatenate.13), calls=%async_computation.1 | async-start | bytes 4194304 | tf_op jit(solution)/shard_map/all_to_all | solution.py:21
  149.1 114.0 %copy-start = (bf16[3,1,256,256]{3,2,1,0:T(8,128)(2,1)S(1)}, bf16[3,1,256,256]{3,2,1,0:T(8,128)(2,1)}, u32[]{:S(2)}) copy-start(bf16[3,1,256,256]{3,2,1,0:T(8,128)(2,1)} %param.10) | copy-start | bytes 1179652
  149.1 112.8 %all-reduce.7.cloned.1.call-start = ((), (), s32[]{:S(2)}) async-start(), calls=%async_computation.5 | async-start | bytes 262144 | tf_op jit(solution)/shard_map/psum | solution.py:15
  265.2 57.8 %all-to-all-start.2 = ((bf16[32,256,128]{2,1,0:T(8,128)(2,1)}), bf16[32,256,128]{2,1,0:T(8,128)(2,1)S(1)}, u32[]{:S(2)}, u32[]{:S(2)}) async-start(bf16[32,256,128]{2,1,0:T(8,128)(2,1)} %concatenate.14), calls=%async_computation.2 | async-start | bytes 4194304 | tf_op jit(solution)/shard_map/all_to_all | solution.py:21
  275.4 112.8 %all-reduce.9.cloned.1.call-start = ((), (), s32[]{:S(2)}) async-start(), calls=%async_computation.6 | async-start | bytes 262144 | tf_op jit(solution)/shard_map/psum | solution.py:15
  391.3 57.8 %all-to-all-start.3 = ((bf16[32,256,128]{2,1,0:T(8,128)(2,1)}), bf16[32,256,128]{2,1,0:T(8,128)(2,1)S(1)}, u32[]{:S(2)}, u32[]{:S(2)}) async-start(bf16[32,256,128]{2,1,0:T(8,128)(2,1)} %concatenate.15), calls=%async_computation.3 | async-start | bytes 4194304 | tf_op jit(solution)/shard_map/all_to_all | solution.py:21
  401.5 114.1 %all-reduce.11.cloned.1.call-start = ((), (), s32[]{:S(2)}) async-start(), calls=%async_computation.7 | async-start | bytes 262144 | tf_op jit(solution)/shard_map/psum | solution.py:15
Sparse Core Ops, SparseCore 0:
  72.8 62.9 all-reduce.4
  198.9 62.8 all-reduce.6
  325.3 62.8 all-reduce.8
  452.7 62.8 all-reduce.10
